TPU v7x, 256 devices: a whole 4x4x8 slice. The times are simulated.
256 devices in a mesh: head: 32 (over y, z_hi, core), dp: 8 (over z_lo, x).
Axes of the slice: x: 4, y: 4, z: 8 (z_hi: 4, z_lo: 2; z = z_hi * 2 + z_lo), core: 2. Of those that a mesh axis runs over, the one named last changes fastest.
Arguments:
- gradient_part: bfloat16 [8, 3, 4608, 4096], P('dp', None, None, 'head'), may hold values from -15 to 15
- carried_error: bfloat16 [8, 3, 4608, 4096], P('dp', None, None, 'head'), may hold values from -4 to 4
- query_basis: float32 [4096, 4], P('head'), may hold values from -6 to 6
Outputs:
- new_error: bfloat16 [8, 3, 4608, 4096], P('dp', None, None, 'head')
- compressed: float32 [4096, 4], P('head')
All inputs are finite; a program needn't handle non-finite values.
Results may differ from a plain program's by a relative error of at most 0.008.
Values may be sent and summed in bfloat16 or wider, within the bound.
A program may use at most 64 MiB of HBM per device.

v0:
```python
import jax
import jax.numpy as jnp
from jax import lax
from jax.sharding import PartitionSpec as P


def copy_for_each(array, axis):
    size = lax.axis_size(axis)
    return lax.all_to_all(
        jnp.broadcast_to(array[None], (size, *array.shape)), axis, 0, 0, tiled=True
    )


def over_copies(array, axis):
    everything = copy_for_each(array, axis)
    return jnp.sum(everything, axis=0)


def cut_along(array, dim, size):
    shape = array.shape
    pieces = array.reshape(*shape[:dim], size, shape[dim] // size, *shape[dim + 1 :])
    return jnp.moveaxis(pieces, dim, 0)


def sum_at_owner(array, axis, dim):
    pieces = cut_along(array, dim, lax.axis_size(axis))
    arrived = lax.all_to_all(pieces, axis, split_axis=0, concat_axis=0, tiled=True)
    return arrived.astype(jnp.float32).sum(axis=0)


def joined_along(pieces, dim):
    shape = list(pieces.shape[1:])
    shape[dim] *= pieces.shape[0]
    return jnp.moveaxis(pieces, 0, dim).reshape(shape)


def gathered_copies(array, axis, dim):
    return joined_along(copy_for_each(array, axis), dim)


def orthonormalize(projected):
    gram = over_copies(jnp.dot(projected.T, projected, precision=lax.Precision.HIGHEST), "head")
    lower_factor = jnp.linalg.cholesky(gram)
    return jax.scipy.linalg.solve_triangular(lower_factor, projected.T, lower=True).T


def per_device(gradient_part, carried_error, query_basis):
    local_width = gradient_part.shape[3]
    stacked_rows = gradient_part.shape[1] * gradient_part.shape[2]
    flat_gradient = gradient_part.reshape(stacked_rows, local_width)
    flat_error = carried_error.reshape(stacked_rows, local_width)
    replicas = lax.axis_size("dp")
    merged = flat_gradient.astype(jnp.float32) + flat_error.astype(jnp.float32)
    partial_rows = sum_at_owner(
        jnp.dot(merged, query_basis, precision=lax.Precision.HIGHEST).astype(jnp.bfloat16),
        "head",
        0,
    )
    projected = over_copies(partial_rows, "dp")
    basis = orthonormalize(projected)
    whole_basis = gathered_copies(basis, "head", 0)
    factor_terms = jnp.dot(merged.T, whole_basis, precision=lax.Precision.HIGHEST)
    compressed = over_copies(factor_terms, "dp") / replicas
    returned = (
        merged - jnp.dot(whole_basis, compressed.T, precision=lax.Precision.HIGHEST)
    ).astype(jnp.bfloat16)
    new_error = returned.reshape(gradient_part.shape)
    return (new_error, compressed)


def solution(mesh):
    in_specs = (P("dp", None, None, "head"), P("dp", None, None, "head"), P("head", None))
    out_specs = (P("dp", None, None, "head"), P("head", None))
    return jax.shard_map(
        per_device, mesh=mesh, in_specs=in_specs, out_specs=out_specs, check_vma=False
    )
```

profile of v0, /device:TPU:1, one launch (start us, length us, event | category | flops | bytes accessed | tf_op | source)
XLA Modules:
  0.0 108.1 jit_solution(16879457435953710768)
XLA Ops:
  0.6 0.0 copy-start
  0.6 3.8 %convert_add_fusion = f32[1,3,4608,128]{3,2,1,0:T(8,128)S(1)} fusion(bf16[1,3,4608,128]{3,2,1,0:T(8,128)(2,1)} %param.4, bf16[1,3,4608,128]{3,2,1,0:T(8,128)(2,1)} %param.3), kind=kLoop, calls=%fused_computation.3 | loop fusion | flops 5308416 | bytes 14155776 | tf_op jit(solution)/shard_map/add | solution.py:53
  4.4 0.0 copy-start.1
  4.4 2.9 %copy-done.1 = f32[1,3,4608,128]{3,2,1,0:T(8,128)} copy-done((f32[1,3,4608,128]{3,2,1,0:T(8,128)}, f32[1,3,4608,128]{3,2,1,0:T(8,128)S(1)}, u32[]{:S(2)}) %copy-start.1) | copy-done | bytes 7077912
  7.3 0.0 copy-done
  7.3 6.1 %convolution_convert_fusion = bf16[13824,4]{0,1:T(4,128)(2,1)S(1)} fusion(f32[13824,128]{1,0:T(8,128)S(1)} %bitcast.25, f32[128,4]{0,1:T(4,128)S(1)} %copy-done), kind=kOutput, calls=%fused_computation.2 | convolution fusion | flops 84989952 | bytes 7190528 | tf_op jit(solution)/shard_map/dot_general | solution.py:55
  13.4 0.3 reshape.33
  13.7 0.1 copy.34
  13.8 23.5 %all_to_all.25 = bf16[32,432,4]{1,2,0:T(4,128)(2,1)S(1)} all-to-all(bf16[32,432,4]{1,2,0:T(4,128)(2,1)S(1)} %copy.34), channel_id=1, replica_groups=mesh['head'=32,'dp'=8] {'head'}, dimensions={0} | all-to-all | bytes 221184 | tf_op jit(solution)/shard_map/all_to_all | solution.py:27
  37.4 9.5 %all_to_all.26 = f32[8,432,4]{1,2,0:T(4,128)S(1)} all-to-all(f32[8,432,4]{1,2,0:T(4,128)S(1)} %broadcast_in_dim.8), channel_id=1, replica_groups=mesh['head'=32,'dp'=8] {'dp'}, dimensions={0} | all-to-all | bytes 110592 | tf_op jit(solution)/shard_map/all_to_all | solution.py:9
  46.9 0.1 fusion.5
  47.1 14.3 %all_to_all.27 = f32[32,4,4]{2,1,0:T(4,128)S(1)} all-to-all(f32[32,4,4]{2,1,0:T(4,128)S(1)} %broadcast_in_dim.9), channel_id=1, replica_groups=mesh['head'=32,'dp'=8] {'head'}, dimensions={0} | all-to-all | bytes 4096 | tf_op jit(solution)/shard_map/all_to_all | solution.py:9
  61.4 0.1 copy.37
  61.5 0.4 cholesky.16
  61.9 0.6 compare_reduce_fusion
  62.5 0.6 fusion.1
  63.2 0.3 custom-call.7
  63.5 0.2 fusion.2
  63.8 16.3 %all_to_all.28 = f32[32,432,4]{1,2,0:T(4,128)S(1)} all-to-all(f32[32,432,4]{1,2,0:T(4,128)S(1)} %broadcast_in_dim.10), channel_id=1, replica_groups=mesh['head'=32,'dp'=8] {'head'}, dimensions={0} | all-to-all | bytes 442368 | tf_op jit(solution)/shard_map/all_to_all | solution.py:9
  80.1 0.1 copy.39
  80.2 0.3 reshape.34
  80.5 5.9 %fusion.6 = f32[128,4]{0,1:T(4,128)S(1)} fusion(f32[13824,128]{1,0:T(8,128)} %bitcast.26, f32[13824,4]{0,1:T(4,128)S(1)} %reshape.34), kind=kOutput, calls=%fused_computation.17 | convolution fusion | flops 84934656 | bytes 7301120 | tf_op jit(solution)/shard_map/dot_general | solution.py:62
  86.4 7.4 %all_to_all.29 = f32[8,128,4]{1,2,0:T(4,128)S(1)} all-to-all(f32[8,128,4]{1,2,0:T(4,128)S(1)} %broadcast_in_dim.11), channel_id=1, replica_groups=mesh['head'=32,'dp'=8] {'dp'}, dimensions={0} | all-to-all | bytes 32768 | tf_op jit(solution)/shard_map/all_to_all | solution.py:9
  93.9 0.0 copy-start.2
  93.9 14.3 %fusion = bf16[13824,128]{1,0:T(8,128)(2,1)} fusion(f32[13824,128]{1,0:T(8,128)} %bitcast.27, f32[13824,4]{0,1:T(4,128)S(1)} %reshape.34, f32[128,4]{0,1:T(4,128)S(1)} %broadcast_multiply_fusion), kind=kOutput, calls=%fused_computation.1 | convolution fusion | flops 88473600 | bytes 10840064 | tf_op jit(solution)/shard_map/dot_general | solution.py:65
  108.1 0.0 copy-done.2
  (11 shorter events, 0.3 us)
Async XLA Ops:
  0.6 6.7 %copy-start = (f32[128,4]{0,1:T(4,128)S(1)}, f32[128,4]{0,1:T(4,128)}, u32[]{:S(2)}) copy-start(f32[128,4]{0,1:T(4,128)} %param.5) | copy-start | bytes 6148
  4.4 2.9 %copy-start.1 = (f32[1,3,4608,128]{3,2,1,0:T(8,128)}, f32[1,3,4608,128]{3,2,1,0:T(8,128)S(1)}, u32[]{:S(2)}) copy-start(f32[1,3,4608,128]{3,2,1,0:T(8,128)S(1)} %convert_add_fusion) | copy-start | bytes 21233668
  93.9 14.3 %copy-start.2 = (f32[128,4]{0,1:T(4,128)}, f32[128,4]{0,1:T(4,128)S(1)}, u32[]{:S(2)}) copy-start(f32[128,4]{0,1:T(4,128)S(1)} %broadcast_multiply_fusion) | copy-start | bytes 6148
where the time goes:
time: 108 us
  blocking collectives  71 us (66%)
  matrix products  26.6 us (25%)
  other arithmetic  5.94 us (6%)
  local copies, waits for them, and re-layouts  3.84 us (4%)
    all_to_all x4, blocking collectives, copy_for_each(): lax.all_to_all(jnp.broadcast_to(array[None], (size, *array.shape)), axis,...  47.5 us
    all_to_all x1, blocking collectives, sum_at_owner(): lax.all_to_all(pieces, axis, split_axis=0, concat_axis=0, tiled=True)  23.5 us
    dot_general x1, matrix products, per_device(): jnp.dot(whole_basis, compressed.T, precision=lax.Precision.HIGHEST)  14.3 us
    dot_general x1, matrix products, per_device(): jnp.dot(merged, query_basis, precision=lax.Precision.HIGHEST)  6.05 us
    dot_general x1, matrix products, per_device(): jnp.dot(merged.T, whole_basis, precision=lax.Precision.HIGHEST)  5.94 us
    add x1, other arithmetic, per_device(): merged = flat_gradient.astype(jnp.float32) + flat_error.astype(jnp.float32)  3.77 us
    unnamed x6, local copies, waits for them, and re-layouts  2.92 us

commit v1 on v0

v1 whole, which is shorter than its diff:
```python
import functools

import jax
import jax.numpy as jnp
from jax import lax
from jax.experimental import pallas as pl
from jax.experimental.pallas import tpu as pltpu
from jax.sharding import PartitionSpec as P

MESH = pl.DeviceIdType.MESH
RANK = 4
LANES = 128
BLOCKS = 4
CHUNK = BLOCKS * LANES
TILE = BLOCKS * RANK
GROUP = 3
PLANE = 32
DEPTH = 8
REPLICAS = 8
FAR_FIRST = (2, 1, 3)


def rem(a, b):
    return lax.rem(a, jnp.int32(b))


def div(a, b):
    return lax.div(a, jnp.int32(b))


def place():
    head, dp = lax.axis_index("head"), lax.axis_index("dp")
    core, z_hi, y = rem(head, 2), rem(div(head, 2), 4), div(head, 8)
    x, z_lo = rem(dp, 4), div(dp, 4)
    return y, x, core, z_hi * 2 + z_lo


def device(y, x, core, z):
    return {"head": (y * 4 + div(z, 2)) * 2 + core, "dp": rem(z, 2) * 4 + x}


def of_plane(index, z):
    return device(div(index, 8), rem(div(index, 2), 4), rem(index, 2), z)


def column_rows(shape):
    return lax.broadcasted_iota(jnp.int32, shape, 0)


def inverse_factor(gram):
    rows, columns = column_rows(gram.shape), lax.broadcasted_iota(jnp.int32, gram.shape, 1)

    def entry(j, k):
        picked = (rows - columns == j - k) & ((rows & 3) == j) & ((columns & 3) == k)
        return jnp.sum(jnp.where(picked, gram, 0.0), axis=(0, 1), keepdims=True)

    lower, inverse = {}, []
    for j in range(RANK):
        for k in range(j):
            total = entry(j, k)
            for i in range(k):
                total = total - lower[j, i] * lower[k, i]
            lower[j, k] = total * inverse[k]
        total = entry(j, j)
        for i in range(j):
            total = total - lower[j, i] * lower[j, i]
        inverse.append(1.0 / jnp.sqrt(total))
    return lower, inverse


def factor_kernel(
    chunks, g_hbm, e_hbm, q_ref, m_ref, left_ref, right_ref, factor_ref,
    g, e, outgoing, arrived, deep, whole, terms,
    load_sem, rs_send, rs_recv, z_send, z_recv, ag_send, ag_recv, dp_send, dp_recv,
):
    y, x, core, z = place()
    me = (y * 4 + x) * 2 + core
    dp = rem(z, 2) * 4 + x
    owner = me < chunks
    groups = chunks // GROUP
    first_group = rem(me, groups)

    def group_at(step):
        return rem(first_group + step, groups)

    def loads(step):
        at = pl.ds(group_at(step) * GROUP, GROUP)
        return [
            pltpu.make_async_copy(src.at[at], dst.at[at], load_sem.at[i, group_at(step)])
            for i, (src, dst) in enumerate(((g_hbm, g), (e_hbm, e)))
        ]

    def start_loads(step, carry):
        for copy in loads(step):
            copy.start()
        return carry

    lax.fori_loop(0, groups, start_loads, 0)

    barrier = pltpu.get_barrier_semaphore()

    def greet(step, carry):
        pl.semaphore_signal(
            barrier, inc=1, device_id=of_plane(rem(me + step, PLANE), z), device_id_type=MESH
        )
        return carry

    lax.fori_loop(1, PLANE, greet, 0)
    for step in range(1, DEPTH):
        pl.semaphore_signal(
            barrier, inc=1, device_id=device(y, x, core, rem(z + step, DEPTH)), device_id_type=MESH
        )
    z_other = div(z, 2) * 2 + 1 - rem(z, 2)
    for step in range(1, 4):
        pl.semaphore_signal(
            barrier, inc=1, device_id=device(y, rem(x + step, 4), core, z_other), device_id_type=MESH
        )

    q = q_ref[...]
    high = q.astype(jnp.bfloat16).astype(jnp.float32)
    both = jnp.concatenate([high, q - high], axis=0)
    q_rows = jnp.concatenate([both, both], axis=1).astype(jnp.bfloat16)
    upper = column_rows((2 * RANK, LANES)) < RANK

    def project(step, carry):
        for copy in loads(step):
            copy.wait()
        base = group_at(step) * GROUP
        at = pl.ds(base, GROUP)
        rows = GROUP * CHUNK
        merged = jnp.concatenate(
            [g[at].reshape(rows, LANES), e[at].reshape(rows, LANES)], axis=1
        )
        product = lax.dot_general(
            q_rows, merged, (((1,), (1,)), ((), ())), preferred_element_type=jnp.float32
        )
        total = product + pltpu.roll(product, RANK, 0)
        for i in range(GROUP):
            starts = [i * CHUNK + b * LANES for b in range(BLOCKS)]
            pieces = [total[:, start : start + LANES] for start in starts]
            tile = jnp.concatenate(
                [jnp.where(upper, pieces[0], pieces[1]), jnp.where(upper, pieces[2], pieces[3])], axis=0
            )
            outgoing[base + i] = tile.astype(jnp.bfloat16)
        return carry

    lax.fori_loop(0, groups, project, 0)

    pl.semaphore_wait(barrier, PLANE - 1 + DEPTH - 1 + 3)

    def send_terms(step, carry):
        chunk = rem(me + step, PLANE)

        @pl.when(chunk < chunks)
        def _():
            pltpu.make_async_remote_copy(
                src_ref=outgoing.at[chunk], dst_ref=arrived.at[me], send_sem=rs_send, recv_sem=rs_recv,
                device_id=of_plane(chunk, z), device_id_type=MESH,
            ).start()

        return carry

    lax.fori_loop(1, PLANE, send_terms, 0)

    @pl.when(owner)
    def _():
        arrived[me] = outgoing[me]

    def merge(chunk, carry):
        m_ref[chunk] = g[chunk].astype(jnp.float32) + e[chunk].astype(jnp.float32)
        return carry

    lax.fori_loop(0, chunks, merge, 0)

    def wait_bytes(ref, count, sem):
        at = ref.at[pl.ds(0, count)]
        pltpu.make_async_copy(at, at, sem).wait()

    @pl.when(owner)
    def _():
        wait_bytes(arrived, PLANE - 1, rs_recv)
        total = arrived[0].astype(jnp.float32)
        for i in range(1, PLANE):
            total = total + arrived[i].astype(jnp.float32)
        deep[z] = total.astype(jnp.bfloat16)
        for step in (4, 3, 5, 2, 6, 1, 7):
            pltpu.make_async_remote_copy(
                src_ref=deep.at[z], dst_ref=deep.at[z], send_sem=z_send, recv_sem=z_recv,
                device_id=device(y, x, core, rem(z + step, DEPTH)), device_id_type=MESH,
            ).start()
        wait_bytes(deep, DEPTH - 1, z_recv)
        total = deep[0].astype(jnp.float32)
        for i in range(1, DEPTH):
            total = total + deep[i].astype(jnp.float32)
        whole[me] = total.astype(jnp.bfloat16)

        def send_whole(step, carry):
            pltpu.make_async_remote_copy(
                src_ref=whole.at[me], dst_ref=whole.at[me], send_sem=ag_send, recv_sem=ag_recv.at[me],
                device_id=of_plane(rem(me + step, PLANE), z), device_id_type=MESH,
            ).start()
            return carry

        lax.fori_loop(1, PLANE, send_whole, 0)

    block_of = div(column_rows((TILE, LANES)), RANK)
    spans = 3
    span = chunks // spans
    result = jnp.zeros((TILE, 2 * LANES), jnp.float32)
    for part in range(spans):
        def await_whole(i, carry):
            chunk = part * span + i

            @pl.when(chunk != me)
            def _():
                pltpu.make_async_copy(whole.at[chunk], whole.at[chunk], ag_recv.at[chunk]).wait()

            return carry

        lax.fori_loop(0, span, await_whole, 0)
        at = slice(part * span, (part + 1) * span)
        left = []
        for chunk in range(part * span, (part + 1) * span):
            tile = whole[chunk].astype(jnp.float32)
            left += [jnp.where(block_of == b, tile, 0.0).astype(jnp.bfloat16) for b in range(BLOCKS)]
        right = jnp.concatenate(
            [g[at].reshape(span * CHUNK, LANES), e[at].reshape(span * CHUNK, LANES)], axis=1
        )
        result = result + jnp.dot(
            jnp.concatenate(left, axis=1), right, preferred_element_type=jnp.float32
        )

    half = result[:, :LANES] + result[:, LANES:]
    half = half[: 2 * RANK] + half[2 * RANK :]
    terms[dp] = half + pltpu.roll(half, RANK, 0)
    for step in (2, 1, 3, 0):
        for flip in (1, 0):
            if step == 0 and flip == 0:
                continue
            pltpu.make_async_remote_copy(
                src_ref=terms.at[dp], dst_ref=terms.at[dp], send_sem=dp_send, recv_sem=dp_recv,
                device_id=device(y, rem(x + step, 4), core, z_other if flip else z), device_id_type=MESH,
            ).start()

    tiles = jnp.concatenate([whole[chunk] for chunk in range(chunks)], axis=1)
    gram = lax.dot_general(tiles, tiles, (((1,), (1,)), ((), ())), preferred_element_type=jnp.float32)
    lower, inverse = inverse_factor(gram)

    def turn(step, carry):
        for i in range(GROUP):
            chunk = step * GROUP + i
            tile = whole[chunk].astype(jnp.float32)
            twice = jnp.concatenate([tile, tile], axis=0)
            left_ref[chunk] = twice.T.astype(jnp.bfloat16)
        return carry

    lax.fori_loop(0, groups, turn, 0)

    wait_bytes(terms, REPLICAS - 1, dp_recv)
    total = terms[0]
    for i in range(1, REPLICAS):
        total = total + terms[i]
    total = total * (1.0 / REPLICAS)
    columns = []
    for j in range(RANK):
        value = total[j : j + 1, :]
        for k in range(j):
            value = value - lower[j, k] * columns[k]
        columns.append(value * inverse[j])
    weights = [None] * RANK
    for j in reversed(range(RANK)):
        value = columns[j]
        for k in range(j + 1, RANK):
            value = value - lower[k, j] * weights[k]
        weights[j] = value * inverse[j]
    for j in range(RANK):
        factor_ref[j : j + 1, :] = columns[j]
    kind = rem(column_rows((TILE, LANES)), RANK)
    spread = jnp.broadcast_to(weights[0], (TILE, LANES))
    for j in range(1, RANK):
        spread = jnp.where(kind == j, weights[j], spread)
    high = spread.astype(jnp.bfloat16).astype(jnp.float32)
    low = spread - high
    for b in range(BLOCKS):
        at = slice(b * LANES, (b + 1) * LANES)
        pair = [jnp.where(block_of == b, part, 0.0) for part in (high, low)]
        right_ref[:, at] = jnp.concatenate(pair, axis=0).astype(jnp.bfloat16)

    @pl.when(owner)
    def _():
        wait_bytes(outgoing, chunks - 1, rs_send)
        wait_bytes(deep, DEPTH - 1, z_send)
        wait_bytes(arrived, PLANE - 1, ag_send)

    @pl.when(jnp.logical_not(owner))
    def _():
        wait_bytes(outgoing, chunks, rs_send)

    wait_bytes(terms, REPLICAS - 1, dp_send)


def residual_kernel(chunks, m_ref, left_ref, right_ref, out_hbm, out, sem):
    groups = chunks // GROUP

    def stores(step):
        at = pl.ds(step * GROUP, GROUP)
        return pltpu.make_async_copy(out.at[at], out_hbm.at[at], sem.at[step])

    def work(step, carry):
        for i in range(GROUP):
            chunk = step * GROUP + i
            product = jnp.dot(left_ref[chunk], right_ref[...], preferred_element_type=jnp.float32)
            for b in range(BLOCKS):
                at = slice(b * LANES, (b + 1) * LANES)
                out[chunk, at] = (m_ref[chunk, at] - product[:, at]).astype(jnp.bfloat16)
        stores(step).start()
        return carry

    lax.fori_loop(0, groups, work, 0)

    def drain(step, carry):
        stores(step).wait()
        return carry

    lax.fori_loop(0, groups, drain, 0)


def per_device(gradient_part, carried_error, query_basis):
    width = gradient_part.shape[3]
    chunks = gradient_part.shape[1] * gradient_part.shape[2] // CHUNK
    tiled = (chunks, CHUNK, width)
    bf16, f32 = jnp.bfloat16, jnp.float32
    any_space = pl.BlockSpec(memory_space=pl.ANY)
    vmem = pl.BlockSpec(memory_space=pltpu.VMEM)
    dma = pltpu.SemaphoreType.DMA
    merged, left, right, factor = pl.pallas_call(
        functools.partial(factor_kernel, chunks),
        out_shape=(
            pltpu.VMEM(tiled, f32),
            pltpu.VMEM((chunks, LANES, 2 * TILE), bf16),
            pltpu.VMEM((2 * TILE, CHUNK), bf16),
            jax.ShapeDtypeStruct((RANK, width), f32),
        ),
        in_specs=[any_space, any_space, vmem],
        out_specs=(vmem, vmem, vmem, vmem),
        scratch_shapes=[
            pltpu.VMEM(tiled, bf16),
            pltpu.VMEM(tiled, bf16),
            pltpu.VMEM((chunks, TILE, LANES), bf16),
            pltpu.VMEM((PLANE, TILE, LANES), bf16),
            pltpu.VMEM((DEPTH, TILE, LANES), bf16),
            pltpu.VMEM((chunks, TILE, LANES), bf16),
            pltpu.VMEM((REPLICAS, 2 * RANK, LANES), f32),
            dma((2, chunks // GROUP)),
            dma, dma, dma, dma, dma,
            dma((chunks,)),
            dma, dma,
        ],
        compiler_params=pltpu.CompilerParams(
            collective_id=0, has_side_effects=True, vmem_limit_bytes=24 << 20
        ),
        name="factor",
    )(gradient_part.reshape(tiled), carried_error.reshape(tiled), query_basis.T)
    returned = pl.pallas_call(
        functools.partial(residual_kernel, chunks),
        out_shape=jax.ShapeDtypeStruct(tiled, bf16),
        in_specs=[vmem, vmem, vmem],
        out_specs=any_space,
        scratch_shapes=[pltpu.VMEM(tiled, bf16), dma((chunks // GROUP,))],
        compiler_params=pltpu.CompilerParams(vmem_limit_bytes=16 << 20),
        name="residual",
    )(merged, left, right)
    return returned.reshape(gradient_part.shape), factor.T


def solution(mesh):
    in_specs = (P("dp", None, None, "head"), P("dp", None, None, "head"), P("head", None))
    out_specs = (P("dp", None, None, "head"), P("head", None))
    return jax.shard_map(
        per_device, mesh=mesh, in_specs=in_specs, out_specs=out_specs, check_vma=False
    )
```

time: 108 us -> 43.9 us (0.41)
  blocking collectives: 71 us -> 0 us
  Pallas kernels: 0 us -> 37.8 us
  matrix products: 26.6 us -> 0 us
  other arithmetic: 5.94 us -> 0 us
  local copies, waits for them, and re-layouts: 3.84 us -> 5.26 us
    all_to_all x5 -> x0, blocking collectives: 71 us -> none  [the longest x4 47.5 us: copy_for_each(): lax.all_to_all(jnp.broadcast_to(array[None], (size, *array.shape)), axis,...]
    pallas_call x0 -> x2, Pallas kernels: none -> 37.8 us  [the longest x1 34.8 us: per_device(): pl.pallas_call(functools.partial(factor_kernel, chunks), out_shape=(pltpu...]
    dot_general x4 -> x0, matrix products: 26.4 us -> none  [the longest x1 14.3 us: per_device(): jnp.dot(whole_basis, compressed.T, precision=lax.Precision.HIGHEST)]
    add x1 -> x0, other arithmetic: 3.77 us -> none  [per_device(): merged = flat_gradient.astype(jnp.float32) + flat_error.astype(jnp.float32)]
    unnamed x6 -> x7, local copies, waits for them, and re-layouts: 2.92 us -> 5.26 us
    another operation x5 -> x0, other arithmetic: 2.02 us -> none  [the longest x3 1.03 us: orthonormalize(): lower_factor = jnp.linalg.cholesky(gram)]
where the time goes in v1:
time: 43.9 us; the launch traced here: 43.7 us
  Pallas kernels  37.8 us (86%)
  local copies, waits for them, and re-layouts  5.26 us (12%)
  between operations  0.66 us (2%)
    pallas_call x1, Pallas kernels, per_device(): pl.pallas_call(functools.partial(factor_kernel, chunks), out_shape=(pltpu...  34.8 us
    unnamed x7, local copies, waits for them, and re-layouts  5.26 us
    pallas_call x1, Pallas kernels, per_device(): pl.pallas_call(functools.partial(residual_kernel, chunks), out_shape=jax....  2.97 us

profile of v1, /device:TPU:1, one launch (start us, length us, event | category | flops | bytes accessed | tf_op | source)
XLA Modules:
  0.0 43.7 jit_solution(6749379233310416321)
XLA Ops:
  0.6 0.0 copy-start
  0.6 2.0 %copy-done = bf16[1,3,4608,128]{3,2,1,0:T(8,128)(2,1)S(1)} copy-done((bf16[1,3,4608,128]{3,2,1,0:T(8,128)(2,1)S(1)}, bf16[1,3,4608,128]{3,2,1,0:T(8,128)(2,1)}, u32[]{:S(2)}) %copy-start) | copy-done | bytes 3538968
  2.6 0.0 copy-start.1
  2.6 2.0 %copy-done.1 = bf16[1,3,4608,128]{3,2,1,0:T(8,128)(2,1)S(1)} copy-done((bf16[1,3,4608,128]{3,2,1,0:T(8,128)(2,1)S(1)}, bf16[1,3,4608,128]{3,2,1,0:T(8,128)(2,1)}, u32[]{:S(2)}) %copy-start.1) | copy-done | bytes 3538968
  4.6 0.0 copy-start.2
  4.6 0.7 %copy-done.2 = f32[128,4]{0,1:T(4,128)S(1)} copy-done((f32[128,4]{0,1:T(4,128)S(1)}, f32[128,4]{0,1:T(4,128)}, u32[]{:S(2)}) %copy-start.2) | copy-done | bytes 2072
  5.3 34.8 %factor.1 = (f32[27,512,128]{2,1,0:T(8,128)S(1)}, bf16[27,128,32]{2,1,0:T(8,128)(2,1)S(1)}, bf16[32,512]{1,0:T(8,128)(2,1)S(1)}, f32[4,128]{1,0:T(4,128)S(1)}) custom-call(bf16[27,512,128]{2,1,0:T(8,128)(2,1)S(1)} %bitcast.5, bf16[27,512,128]{2,1,0:T(8,128)(2,1)S(1)} %bitcast.6, f32[4,128]{1,0:T(4,128)S(1)} %bitcast.8), custom_call_target="tpu_custom_call" | custom-call | tf_op jit(solution)/shard_map/factor/pallas_call | solution.py:336
  40.1 3.0 %residual.1 = bf16[27,512,128]{2,1,0:T(8,128)(2,1)} custom-call(f32[27,512,128]{2,1,0:T(8,128)S(1)} %get-tuple-element.6.m_ref, bf16[27,128,32]{2,1,0:T(8,128)(2,1)S(1)} %get-tuple-element.7.left_ref, bf16[32,512]{1,0:T(8,128)(2,1)S(1)} %get-tuple-element.8.right_ref), custom_call_target="tpu_custom_call" | custom-call | tf_op jit(solution)/shard_map/residual/pallas_call | solution.py:364
  43.1 0.6 %copy.6 = f32[128,4]{0,1:T(4,128)} copy(f32[128,4]{0,1:T(4,128)S(1)} %bitcast.7) | data formatting | bytes 4096
Async XLA Ops:
  0.6 2.0 %copy-start = (bf16[1,3,4608,128]{3,2,1,0:T(8,128)(2,1)S(1)}, bf16[1,3,4608,128]{3,2,1,0:T(8,128)(2,1)}, u32[]{:S(2)}) copy-start(bf16[1,3,4608,128]{3,2,1,0:T(8,128)(2,1)} %param.3) | copy-start | bytes 10616836
  2.6 2.0 %copy-start.1 = (bf16[1,3,4608,128]{3,2,1,0:T(8,128)(2,1)S(1)}, bf16[1,3,4608,128]{3,2,1,0:T(8,128)(2,1)}, u32[]{:S(2)}) copy-start(bf16[1,3,4608,128]{3,2,1,0:T(8,128)(2,1)} %param.4) | copy-start | bytes 10616836
  4.6 0.7 %copy-start.2 = (f32[128,4]{0,1:T(4,128)S(1)}, f32[128,4]{0,1:T(4,128)}, u32[]{:S(2)}) copy-start(f32[128,4]{0,1:T(4,128)} %param.5) | copy-start | bytes 6148

commit v2 on v1

--- a/solution.py
+++ b/solution.py
@@ -69,9 +69,9 @@
 
 
 def factor_kernel(
-    chunks, g_hbm, e_hbm, q_ref, m_ref, left_ref, right_ref, factor_ref,
-    g, e, outgoing, arrived, deep, whole, terms,
-    load_sem, rs_send, rs_recv, z_send, z_recv, ag_send, ag_recv, dp_send, dp_recv,
+    chunks, g_hbm, e_hbm, q_hbm, m_ref, left_ref, right_ref, factor_ref,
+    g, e, q_ref, outgoing, arrived, deep, whole, terms,
+    load_sem, q_sem, rs_send, rs_recv, z_send, z_recv, ag_send, ag_recv, dp_send, dp_recv,
 ):
     y, x, core, z = place()
     me = (y * 4 + x) * 2 + core
@@ -95,8 +95,7 @@
             copy.start()
         return carry
 
-    lax.fori_loop(0, groups, start_loads, 0)
-
+    q_copy = pltpu.make_async_copy(q_hbm, q_ref, q_sem)
     barrier = pltpu.get_barrier_semaphore()
 
     def greet(step, carry):
@@ -116,6 +115,10 @@
             barrier, inc=1, device_id=device(y, rem(x + step, 4), core, z_other), device_id_type=MESH
         )
 
+    q_copy.start()
+    lax.fori_loop(0, groups, start_loads, 0)
+
+    q_copy.wait()
     q = q_ref[...]
     high = q.astype(jnp.bfloat16).astype(jnp.float32)
     both = jnp.concatenate([high, q - high], axis=0)
@@ -299,8 +302,10 @@
     wait_bytes(terms, REPLICAS - 1, dp_send)
 
 
-def residual_kernel(chunks, m_ref, left_ref, right_ref, out_hbm, out, sem):
+def residual_kernel(chunks, m_ref, left_ref, right_ref, factor_ref, out_hbm, factor_hbm, out, sem, factor_sem):
     groups = chunks // GROUP
+    factor_copy = pltpu.make_async_copy(factor_ref, factor_hbm, factor_sem)
+    factor_copy.start()
 
     def stores(step):
         at = pl.ds(step * GROUP, GROUP)
@@ -323,6 +328,7 @@
         return carry
 
     lax.fori_loop(0, groups, drain, 0)
+    factor_copy.wait()
 
 
 def per_device(gradient_part, carried_error, query_basis):
@@ -330,29 +336,32 @@
     chunks = gradient_part.shape[1] * gradient_part.shape[2] // CHUNK
     tiled = (chunks, CHUNK, width)
     bf16, f32 = jnp.bfloat16, jnp.float32
-    any_space = pl.BlockSpec(memory_space=pl.ANY)
+    hbm = pl.BlockSpec(memory_space=pltpu.HBM)
     vmem = pl.BlockSpec(memory_space=pltpu.VMEM)
     dma = pltpu.SemaphoreType.DMA
+    operands = gradient_part.reshape(tiled), carried_error.reshape(tiled), query_basis.T
+    operands = [pltpu.with_memory_space_constraint(operand, pltpu.HBM) for operand in operands]
     merged, left, right, factor = pl.pallas_call(
         functools.partial(factor_kernel, chunks),
         out_shape=(
             pltpu.VMEM(tiled, f32),
             pltpu.VMEM((chunks, LANES, 2 * TILE), bf16),
             pltpu.VMEM((2 * TILE, CHUNK), bf16),
-            jax.ShapeDtypeStruct((RANK, width), f32),
+            pltpu.VMEM((RANK, width), f32),
         ),
-        in_specs=[any_space, any_space, vmem],
+        in_specs=[hbm, hbm, hbm],
         out_specs=(vmem, vmem, vmem, vmem),
         scratch_shapes=[
             pltpu.VMEM(tiled, bf16),
             pltpu.VMEM(tiled, bf16),
+            pltpu.VMEM((RANK, width), f32),
             pltpu.VMEM((chunks, TILE, LANES), bf16),
             pltpu.VMEM((PLANE, TILE, LANES), bf16),
             pltpu.VMEM((DEPTH, TILE, LANES), bf16),
             pltpu.VMEM((chunks, TILE, LANES), bf16),
             pltpu.VMEM((REPLICAS, 2 * RANK, LANES), f32),
             dma((2, chunks // GROUP)),
-            dma, dma, dma, dma, dma,
+            dma, dma, dma, dma, dma, dma,
             dma((chunks,)),
             dma, dma,
         ],
@@ -360,16 +369,16 @@
             collective_id=0, has_side_effects=True, vmem_limit_bytes=24 << 20
         ),
         name="factor",
-    )(gradient_part.reshape(tiled), carried_error.reshape(tiled), query_basis.T)
-    returned = pl.pallas_call(
+    )(*operands)
+    returned, factor = pl.pallas_call(
         functools.partial(residual_kernel, chunks),
-        out_shape=jax.ShapeDtypeStruct(tiled, bf16),
-        in_specs=[vmem, vmem, vmem],
-        out_specs=any_space,
-        scratch_shapes=[pltpu.VMEM(tiled, bf16), dma((chunks // GROUP,))],
+        out_shape=(pltpu.HBM(tiled, bf16), pltpu.HBM((RANK, width), f32)),
+        in_specs=[vmem, vmem, vmem, vmem],
+        out_specs=(hbm, hbm),
+        scratch_shapes=[pltpu.VMEM(tiled, bf16), dma((chunks // GROUP,)), dma],
         compiler_params=pltpu.CompilerParams(vmem_limit_bytes=16 << 20),
         name="residual",
-    )(merged, left, right)
+    )(merged, left, right, factor)
     return returned.reshape(gradient_part.shape), factor.T
 
 

time: 43.9 us -> 36.2 us (0.82)
  local copies, waits for them, and re-layouts: 5.26 us -> 0 us
  Pallas kernels: 37.8 us -> 35.4 us
    unnamed x7 -> x0, local copies, waits for them, and re-layouts: 5.26 us -> none
    pallas_call x1, Pallas kernels: 34.8 us -> 32.4 us  [per_device(): pl.pallas_call(functools.partial(factor_kernel, chunks), out_shape=(pltpu...]
where the time goes in v2:
time: 36.2 us; the launch traced here: 36.1 us
  Pallas kernels  35.4 us (98%)
  between operations  0.64 us (2%)
    pallas_call x1, Pallas kernels, per_device(): pl.pallas_call(functools.partial(factor_kernel, chunks), out_shape=(pltpu...  32.4 us
    pallas_call x1, Pallas kernels, per_device(): pl.pallas_call(functools.partial(residual_kernel, chunks), out_shape=(plt...  2.98 us

profile of v2, /device:TPU:1, one launch (start us, length us, event | category | flops | bytes accessed | tf_op | source)
XLA Modules:
  0.0 36.1 jit_solution(4055424576778441135)
XLA Ops:
  0.6 32.4 %factor.1 = (f32[27,512,128]{2,1,0:T(8,128)S(1)}, bf16[27,128,32]{2,1,0:T(8,128)(2,1)S(1)}, bf16[32,512]{1,0:T(8,128)(2,1)S(1)}, f32[4,128]{1,0:T(4,128)S(1)}) custom-call(bf16[27,512,128]{2,1,0:T(8,128)(2,1)} %bitcast.5, bf16[27,512,128]{2,1,0:T(8,128)(2,1)} %bitcast.6, f32[4,128]{1,0:T(4,128)} %bitcast.7), custom_call_target="tpu_custom_call" | custom-call | tf_op jit(solution)/shard_map/factor/pallas_call | solution.py:344
  33.1 3.0 %residual.1 = (bf16[27,512,128]{2,1,0:T(8,128)(2,1)}, f32[4,128]{1,0:T(4,128)}) custom-call(f32[27,512,128]{2,1,0:T(8,128)S(1)} %get-tuple-element.8.m_ref, bf16[27,128,32]{2,1,0:T(8,128)(2,1)S(1)} %get-tuple-element.9.left_ref, bf16[32,512]{1,0:T(8,128)(2,1)S(1)} %get-tuple-element.10.right_ref, f32[4,128]{1,0:T(4,128)S(1)} %get-tuple-element.11.factor_ref), custom_call_target="tpu_custom_call" | custom-call | tf_op jit(solution)/shard_map/residual/pallas_call | solution.py:373

commit v3 on v2

--- a/solution.py
+++ b/solution.py
@@ -1,4 +1,5 @@
 import functools
+import itertools
 
 import jax
 import jax.numpy as jnp
@@ -17,7 +18,11 @@
 PLANE = 32
 DEPTH = 8
 REPLICAS = 8
-FAR_FIRST = (2, 1, 3)
+EARLY = 6
+
+
+def wrap(a, b):
+    return jnp.where(a >= b, a - b, a)
 
 
 def rem(a, b):
@@ -70,7 +75,7 @@
 
 def factor_kernel(
     chunks, g_hbm, e_hbm, q_hbm, m_ref, left_ref, right_ref, factor_ref,
-    g, e, q_ref, outgoing, arrived, deep, whole, terms,
+    g, e, q_ref, outgoing, arrived, deep, whole, terms, result_ref,
     load_sem, q_sem, rs_send, rs_recv, z_send, z_recv, ag_send, ag_recv, dp_send, dp_recv,
 ):
     y, x, core, z = place()
@@ -78,45 +83,41 @@
     dp = rem(z, 2) * 4 + x
     owner = me < chunks
     groups = chunks // GROUP
-    first_group = rem(me, groups)
+    first_group = wrap(div(me, GROUP) + 1, groups)
+    first_group = wrap(first_group, groups)
 
     def group_at(step):
-        return rem(first_group + step, groups)
+        return wrap(first_group + step, groups)
 
     def loads(step):
         at = pl.ds(group_at(step) * GROUP, GROUP)
         return [
-            pltpu.make_async_copy(src.at[at], dst.at[at], load_sem.at[i, group_at(step)])
+            pltpu.make_async_copy(src.at[at], dst.at[at], load_sem.at[i, step])
             for i, (src, dst) in enumerate(((g_hbm, g), (e_hbm, e)))
         ]
 
-    def start_loads(step, carry):
+    q_copy = pltpu.make_async_copy(q_hbm, q_ref, q_sem)
+    q_copy.start()
+    for step in range(groups):
         for copy in loads(step):
             copy.start()
-        return carry
-
-    q_copy = pltpu.make_async_copy(q_hbm, q_ref, q_sem)
+
+    ys = [y] + [wrap(y + step, 4) for step in range(1, 4)]
+    xs = [x] + [wrap(x + step, 4) for step in range(1, 4)]
+    cores = [core, 1 - core]
+    zs = [z] + [wrap(z + step, DEPTH) for step in range(1, DEPTH)]
+    z_other = div(z, 2) * 2 + 1 - rem(z, 2)
+    far_first = lambda steps, sizes: -sum(min(step, size - step) for step, size in zip(steps, sizes))
+    plane = sorted(itertools.product(range(4), range(4), range(2)), key=lambda s: far_first(s, (4, 4, 2)))[:-1]
+    line = sorted(range(1, DEPTH), key=lambda s: far_first((s,), (DEPTH,)))
+    plane = [device(ys[i], xs[j], cores[k], z) for i, j, k in plane]
+    line = [device(y, x, core, zs[step]) for step in line]
+    beside = [device(y, xs[step], core, z_other) for step in (2, 1, 3)]
+
     barrier = pltpu.get_barrier_semaphore()
-
-    def greet(step, carry):
-        pl.semaphore_signal(
-            barrier, inc=1, device_id=of_plane(rem(me + step, PLANE), z), device_id_type=MESH
-        )
-        return carry
-
-    lax.fori_loop(1, PLANE, greet, 0)
-    for step in range(1, DEPTH):
-        pl.semaphore_signal(
-            barrier, inc=1, device_id=device(y, x, core, rem(z + step, DEPTH)), device_id_type=MESH
-        )
-    z_other = div(z, 2) * 2 + 1 - rem(z, 2)
-    for step in range(1, 4):
-        pl.semaphore_signal(
-            barrier, inc=1, device_id=device(y, rem(x + step, 4), core, z_other), device_id_type=MESH
-        )
-
-    q_copy.start()
-    lax.fori_loop(0, groups, start_loads, 0)
+    greeted = plane + line + beside
+    for peer in greeted:
+        pl.semaphore_signal(barrier, inc=1, device_id=peer, device_id_type=MESH)
 
     q_copy.wait()
     q = q_ref[...]
@@ -147,23 +148,25 @@
             outgoing[base + i] = tile.astype(jnp.bfloat16)
         return carry
 
-    lax.fori_loop(0, groups, project, 0)
-
-    pl.semaphore_wait(barrier, PLANE - 1 + DEPTH - 1 + 3)
+    lax.fori_loop(0, EARLY, project, 0)
+
+    pl.semaphore_wait(barrier, len(greeted))
 
     def send_terms(step, carry):
-        chunk = rem(me + step, PLANE)
-
-        @pl.when(chunk < chunks)
-        def _():
-            pltpu.make_async_remote_copy(
-                src_ref=outgoing.at[chunk], dst_ref=arrived.at[me], send_sem=rs_send, recv_sem=rs_recv,
-                device_id=of_plane(chunk, z), device_id_type=MESH,
-            ).start()
-
-        return carry
-
-    lax.fori_loop(1, PLANE, send_terms, 0)
+        for i in range(GROUP):
+            chunk = group_at(step) * GROUP + i
+
+            @pl.when(chunk != me)
+            def _():
+                pltpu.make_async_remote_copy(
+                    src_ref=outgoing.at[chunk], dst_ref=arrived.at[me], send_sem=rs_send, recv_sem=rs_recv,
+                    device_id=of_plane(chunk, z), device_id_type=MESH,
+                ).start()
+
+        return carry
+
+    lax.fori_loop(0, EARLY, send_terms, 0)
+    lax.fori_loop(EARLY, groups, lambda step, carry: send_terms(step, project(step, carry)), 0)
 
     @pl.when(owner)
     def _():
@@ -186,10 +189,10 @@
         for i in range(1, PLANE):
             total = total + arrived[i].astype(jnp.float32)
         deep[z] = total.astype(jnp.bfloat16)
-        for step in (4, 3, 5, 2, 6, 1, 7):
+        for peer in line:
             pltpu.make_async_remote_copy(
                 src_ref=deep.at[z], dst_ref=deep.at[z], send_sem=z_send, recv_sem=z_recv,
-                device_id=device(y, x, core, rem(z + step, DEPTH)), device_id_type=MESH,
+                device_id=peer, device_id_type=MESH,
             ).start()
         wait_bytes(deep, DEPTH - 1, z_recv)
         total = deep[0].astype(jnp.float32)
@@ -197,53 +200,48 @@
             total = total + deep[i].astype(jnp.float32)
         whole[me] = total.astype(jnp.bfloat16)
 
-        def send_whole(step, carry):
+        for peer in plane:
             pltpu.make_async_remote_copy(
                 src_ref=whole.at[me], dst_ref=whole.at[me], send_sem=ag_send, recv_sem=ag_recv.at[me],
-                device_id=of_plane(rem(me + step, PLANE), z), device_id_type=MESH,
+                device_id=peer, device_id_type=MESH,
             ).start()
-            return carry
-
-        lax.fori_loop(1, PLANE, send_whole, 0)
 
     block_of = div(column_rows((TILE, LANES)), RANK)
-    spans = 3
-    span = chunks // spans
-    result = jnp.zeros((TILE, 2 * LANES), jnp.float32)
-    for part in range(spans):
-        def await_whole(i, carry):
-            chunk = part * span + i
-
-            @pl.when(chunk != me)
+    outward = lambda step: wrap(div(step + 1, 2) * (1 - 2 * rem(step, 2)) + groups - 1, groups)
+    result_ref[...] = jnp.zeros_like(result_ref)
+
+    def contract(step, carry):
+        base = group_at(outward(step)) * GROUP
+        left = []
+        for i in range(GROUP):
+            @pl.when(base + i != me)
             def _():
-                pltpu.make_async_copy(whole.at[chunk], whole.at[chunk], ag_recv.at[chunk]).wait()
-
-            return carry
-
-        lax.fori_loop(0, span, await_whole, 0)
-        at = slice(part * span, (part + 1) * span)
-        left = []
-        for chunk in range(part * span, (part + 1) * span):
-            tile = whole[chunk].astype(jnp.float32)
+                pltpu.make_async_copy(whole.at[base + i], whole.at[base + i], ag_recv.at[base + i]).wait()
+
+        for i in range(GROUP):
+            tile = whole[base + i].astype(jnp.float32)
             left += [jnp.where(block_of == b, tile, 0.0).astype(jnp.bfloat16) for b in range(BLOCKS)]
+        at = pl.ds(base, GROUP)
         right = jnp.concatenate(
-            [g[at].reshape(span * CHUNK, LANES), e[at].reshape(span * CHUNK, LANES)], axis=1
+            [part[at].reshape(GROUP * CHUNK, LANES) for part in (g, e)], axis=1
         )
-        result = result + jnp.dot(
+        result_ref[...] += jnp.dot(
             jnp.concatenate(left, axis=1), right, preferred_element_type=jnp.float32
         )
+        return carry
+
+    lax.fori_loop(0, groups, contract, 0)
+    result = result_ref[...]
 
     half = result[:, :LANES] + result[:, LANES:]
     half = half[: 2 * RANK] + half[2 * RANK :]
     terms[dp] = half + pltpu.roll(half, RANK, 0)
-    for step in (2, 1, 3, 0):
-        for flip in (1, 0):
-            if step == 0 and flip == 0:
-                continue
-            pltpu.make_async_remote_copy(
-                src_ref=terms.at[dp], dst_ref=terms.at[dp], send_sem=dp_send, recv_sem=dp_recv,
-                device_id=device(y, rem(x + step, 4), core, z_other if flip else z), device_id_type=MESH,
-            ).start()
+    replicas = beside + [device(y, x, core, z_other)] + [device(y, xs[step], core, z) for step in (2, 1, 3)]
+    for peer in replicas:
+        pltpu.make_async_remote_copy(
+            src_ref=terms.at[dp], dst_ref=terms.at[dp], send_sem=dp_send, recv_sem=dp_recv,
+            device_id=peer, device_id_type=MESH,
+        ).start()
 
     tiles = jnp.concatenate([whole[chunk] for chunk in range(chunks)], axis=1)
     gram = lax.dot_general(tiles, tiles, (((1,), (1,)), ((), ())), preferred_element_type=jnp.float32)
@@ -360,6 +358,7 @@
             pltpu.VMEM((DEPTH, TILE, LANES), bf16),
             pltpu.VMEM((chunks, TILE, LANES), bf16),
             pltpu.VMEM((REPLICAS, 2 * RANK, LANES), f32),
+            pltpu.VMEM((TILE, 2 * LANES), f32),
             dma((2, chunks // GROUP)),
             dma, dma, dma, dma, dma, dma,
             dma((chunks,)),

time: 36.2 us -> 35.5 us (0.981)
  Pallas kernels: 35.4 us -> 34.8 us
    pallas_call x1, Pallas kernels: 32.4 us -> 31.8 us  [per_device(): pl.pallas_call(functools.partial(factor_kernel, chunks), out_shape=(pltpu...]
where the time goes in v3:
time: 35.5 us; the launch traced here: 35.4 us
  Pallas kernels  34.8 us (98%)
  between operations  0.64 us (2%)
    pallas_call x1, Pallas kernels, per_device(): pl.pallas_call(functools.partial(factor_kernel, chunks), out_shape=(pltpu...  31.8 us
    pallas_call x1, Pallas kernels, per_device(): pl.pallas_call(functools.partial(residual_kernel, chunks), out_shape=(plt...  2.98 us

profile of v3, /device:TPU:1, one launch (start us, length us, event | category | flops | bytes accessed | tf_op | source)
XLA Modules:
  0.0 35.4 jit_solution(18083076229239375370)
XLA Ops:
  0.6 31.8 %factor.1 = (f32[27,512,128]{2,1,0:T(8,128)S(1)}, bf16[27,128,32]{2,1,0:T(8,128)(2,1)S(1)}, bf16[32,512]{1,0:T(8,128)(2,1)S(1)}, f32[4,128]{1,0:T(4,128)S(1)}) custom-call(bf16[27,512,128]{2,1,0:T(8,128)(2,1)} %bitcast.5, bf16[27,512,128]{2,1,0:T(8,128)(2,1)} %bitcast.6, f32[4,128]{1,0:T(4,128)} %bitcast.7), custom_call_target="tpu_custom_call" | custom-call | tf_op jit(solution)/shard_map/factor/pallas_call | solution.py:342
  32.5 3.0 %residual.1 = (bf16[27,512,128]{2,1,0:T(8,128)(2,1)}, f32[4,128]{1,0:T(4,128)}) custom-call(f32[27,512,128]{2,1,0:T(8,128)S(1)} %get-tuple-element.8.m_ref, bf16[27,128,32]{2,1,0:T(8,128)(2,1)S(1)} %get-tuple-element.9.left_ref, bf16[32,512]{1,0:T(8,128)(2,1)S(1)} %get-tuple-element.10.right_ref, f32[4,128]{1,0:T(4,128)S(1)} %get-tuple-element.11.factor_ref), custom_call_target="tpu_custom_call" | custom-call | tf_op jit(solution)/shard_map/residual/pallas_call | solution.py:372

commit v4 on v3

--- a/solution.py
+++ b/solution.py
@@ -18,6 +18,8 @@
 PLANE = 32
 DEPTH = 8
 REPLICAS = 8
+AHEAD = 2
+UNROLL = 3
 EARLY = 6
 
 
@@ -75,7 +77,7 @@
 
 def factor_kernel(
     chunks, g_hbm, e_hbm, q_hbm, m_ref, left_ref, right_ref, factor_ref,
-    g, e, q_ref, outgoing, arrived, deep, whole, terms, result_ref,
+    ge, q_ref, outgoing, arrived, deep, whole, terms, result_ref,
     load_sem, q_sem, rs_send, rs_recv, z_send, z_recv, ag_send, ag_recv, dp_send, dp_recv,
 ):
     y, x, core, z = place()
@@ -83,22 +85,35 @@
     dp = rem(z, 2) * 4 + x
     owner = me < chunks
     groups = chunks // GROUP
-    first_group = wrap(div(me, GROUP) + 1, groups)
-    first_group = wrap(first_group, groups)
+    own_group = div(me, GROUP)
+    centre = wrap(wrap(own_group, groups), groups)
 
     def group_at(step):
-        return wrap(first_group + step, groups)
+        reach = groups // 2 - div(jnp.int32(step), 2)
+        group = centre + reach * (1 - 2 * rem(jnp.int32(step), 2))
+        return wrap(jnp.where(group < 0, group + groups, group), groups)
 
     def loads(step):
         at = pl.ds(group_at(step) * GROUP, GROUP)
         return [
-            pltpu.make_async_copy(src.at[at], dst.at[at], load_sem.at[i, step])
-            for i, (src, dst) in enumerate(((g_hbm, g), (e_hbm, e)))
+            pltpu.make_async_copy(src.at[at], ge.at[i, at], load_sem.at[step // 2])
+            for i, src in enumerate((g_hbm, e_hbm))
         ]
+
+    def side_by_side(bases):
+        return jnp.concatenate(
+            [
+                jnp.concatenate(
+                    [ge[i, pl.ds(base, GROUP)].reshape(GROUP * CHUNK, LANES) for i in range(2)], axis=1
+                )
+                for base in bases
+            ],
+            axis=0,
+        )
 
     q_copy = pltpu.make_async_copy(q_hbm, q_ref, q_sem)
     q_copy.start()
-    for step in range(groups):
+    for step in range(AHEAD):
         for copy in loads(step):
             copy.start()
 
@@ -120,35 +135,36 @@
         pl.semaphore_signal(barrier, inc=1, device_id=peer, device_id_type=MESH)
 
     q_copy.wait()
+    for step in range(AHEAD, groups):
+        for copy in loads(step):
+            copy.start()
     q = q_ref[...]
     high = q.astype(jnp.bfloat16).astype(jnp.float32)
     both = jnp.concatenate([high, q - high], axis=0)
     q_rows = jnp.concatenate([both, both], axis=1).astype(jnp.bfloat16)
     upper = column_rows((2 * RANK, LANES)) < RANK
 
-    def project(step, carry):
-        for copy in loads(step):
-            copy.wait()
-        base = group_at(step) * GROUP
-        at = pl.ds(base, GROUP)
-        rows = GROUP * CHUNK
-        merged = jnp.concatenate(
-            [g[at].reshape(rows, LANES), e[at].reshape(rows, LANES)], axis=1
-        )
+    def project(pair, count):
+        bases = [group_at(2 * pair + i) * GROUP for i in range(count)]
+        done = ge.at[:, pl.ds(0, count * GROUP)]
+        pltpu.make_async_copy(done, done, load_sem.at[pair]).wait()
         product = lax.dot_general(
-            q_rows, merged, (((1,), (1,)), ((), ())), preferred_element_type=jnp.float32
+            q_rows, side_by_side(bases), (((1,), (1,)), ((), ())), preferred_element_type=jnp.float32
         )
         total = product + pltpu.roll(product, RANK, 0)
-        for i in range(GROUP):
+        for i in range(count * GROUP):
             starts = [i * CHUNK + b * LANES for b in range(BLOCKS)]
             pieces = [total[:, start : start + LANES] for start in starts]
             tile = jnp.concatenate(
                 [jnp.where(upper, pieces[0], pieces[1]), jnp.where(upper, pieces[2], pieces[3])], axis=0
             )
-            outgoing[base + i] = tile.astype(jnp.bfloat16)
-        return carry
-
-    lax.fori_loop(0, EARLY, project, 0)
+            outgoing[bases[i // GROUP] + i % GROUP] = tile.astype(jnp.bfloat16)
+
+    def project_pair(pair, carry):
+        project(pair, 2)
+        return carry
+
+    lax.fori_loop(0, EARLY // 2, project_pair, 0)
 
     pl.semaphore_wait(barrier, len(greeted))
 
@@ -166,14 +182,17 @@
         return carry
 
     lax.fori_loop(0, EARLY, send_terms, 0)
-    lax.fori_loop(EARLY, groups, lambda step, carry: send_terms(step, project(step, carry)), 0)
+    for pair in range(EARLY // 2, pl.cdiv(groups, 2)):
+        count = min(2, groups - 2 * pair)
+        project(pair, count)
+        lax.fori_loop(2 * pair, 2 * pair + count, send_terms, 0)
 
     @pl.when(owner)
     def _():
         arrived[me] = outgoing[me]
 
     def merge(chunk, carry):
-        m_ref[chunk] = g[chunk].astype(jnp.float32) + e[chunk].astype(jnp.float32)
+        m_ref[chunk] = ge[0, chunk].astype(jnp.float32) + ge[1, chunk].astype(jnp.float32)
         return carry
 
     lax.fori_loop(0, chunks, merge, 0)
@@ -202,35 +221,42 @@
 
         for peer in plane:
             pltpu.make_async_remote_copy(
-                src_ref=whole.at[me], dst_ref=whole.at[me], send_sem=ag_send, recv_sem=ag_recv.at[me],
+                src_ref=whole.at[me], dst_ref=whole.at[me], send_sem=ag_send, recv_sem=ag_recv.at[own_group],
                 device_id=peer, device_id_type=MESH,
             ).start()
 
     block_of = div(column_rows((TILE, LANES)), RANK)
-    outward = lambda step: wrap(div(step + 1, 2) * (1 - 2 * rem(step, 2)) + groups - 1, groups)
     result_ref[...] = jnp.zeros_like(result_ref)
 
-    def contract(step, carry):
-        base = group_at(outward(step)) * GROUP
-        left = []
-        for i in range(GROUP):
-            @pl.when(base + i != me)
+    def contract(steps):
+        bases, left = [], []
+        for step in steps:
+            group = group_at(step)
+            bases.append(group * GROUP)
+
+            @pl.when(group == own_group)
             def _():
-                pltpu.make_async_copy(whole.at[base + i], whole.at[base + i], ag_recv.at[base + i]).wait()
-
-        for i in range(GROUP):
-            tile = whole[base + i].astype(jnp.float32)
-            left += [jnp.where(block_of == b, tile, 0.0).astype(jnp.bfloat16) for b in range(BLOCKS)]
-        at = pl.ds(base, GROUP)
-        right = jnp.concatenate(
-            [part[at].reshape(GROUP * CHUNK, LANES) for part in (g, e)], axis=1
+                wait_bytes(whole, GROUP - 1, ag_recv.at[group])
+
+            @pl.when(group != own_group)
+            def _():
+                wait_bytes(whole, GROUP, ag_recv.at[group])
+
+        for base in bases:
+            for i in range(GROUP):
+                tile = whole[base + i].astype(jnp.float32)
+                left += [jnp.where(block_of == b, tile, 0.0).astype(jnp.bfloat16) for b in range(BLOCKS)]
+        result_ref[...] += jnp.dot(
+            jnp.concatenate(left, axis=1), side_by_side(bases), preferred_element_type=jnp.float32
         )
-        result_ref[...] += jnp.dot(
-            jnp.concatenate(left, axis=1), right, preferred_element_type=jnp.float32
-        )
-        return carry
-
-    lax.fori_loop(0, groups, contract, 0)
+
+    def contract_pair(step, carry):
+        pair = groups // 2 - step
+        contract((2 * pair, 2 * pair + 1))
+        return carry
+
+    contract((groups - 1,))
+    lax.fori_loop(1, groups // 2 + 1, contract_pair, 0)
     result = result_ref[...]
 
     half = result[:, :LANES] + result[:, LANES:]
@@ -307,9 +333,14 @@
 
     def stores(step):
         at = pl.ds(step * GROUP, GROUP)
-        return pltpu.make_async_copy(out.at[at], out_hbm.at[at], sem.at[step])
-
-    def work(step, carry):
+        return pltpu.make_async_copy(out.at[at], out_hbm.at[at], sem)
+
+    def work(big, carry):
+        for small in range(UNROLL):
+            one(big * UNROLL + small)
+        return carry
+
+    def one(step):
         for i in range(GROUP):
             chunk = step * GROUP + i
             product = jnp.dot(left_ref[chunk], right_ref[...], preferred_element_type=jnp.float32)
@@ -317,15 +348,10 @@
                 at = slice(b * LANES, (b + 1) * LANES)
                 out[chunk, at] = (m_ref[chunk, at] - product[:, at]).astype(jnp.bfloat16)
         stores(step).start()
-        return carry
-
-    lax.fori_loop(0, groups, work, 0)
-
-    def drain(step, carry):
-        stores(step).wait()
-        return carry
-
-    lax.fori_loop(0, groups, drain, 0)
+
+    lax.fori_loop(0, groups // UNROLL, work, 0)
+
+    pltpu.make_async_copy(out, out_hbm, sem).wait()
     factor_copy.wait()
 
 
@@ -350,8 +376,7 @@
         in_specs=[hbm, hbm, hbm],
         out_specs=(vmem, vmem, vmem, vmem),
         scratch_shapes=[
-            pltpu.VMEM(tiled, bf16),
-            pltpu.VMEM(tiled, bf16),
+            pltpu.VMEM((2, *tiled), bf16),
             pltpu.VMEM((RANK, width), f32),
             pltpu.VMEM((chunks, TILE, LANES), bf16),
             pltpu.VMEM((PLANE, TILE, LANES), bf16),
@@ -359,9 +384,9 @@
             pltpu.VMEM((chunks, TILE, LANES), bf16),
             pltpu.VMEM((REPLICAS, 2 * RANK, LANES), f32),
             pltpu.VMEM((TILE, 2 * LANES), f32),
-            dma((2, chunks // GROUP)),
+            dma((pl.cdiv(chunks // GROUP, 2),)),
             dma, dma, dma, dma, dma, dma,
-            dma((chunks,)),
+            dma((chunks // GROUP,)),
             dma, dma,
         ],
         compiler_params=pltpu.CompilerParams(
@@ -374,7 +399,7 @@
         out_shape=(pltpu.HBM(tiled, bf16), pltpu.HBM((RANK, width), f32)),
         in_specs=[vmem, vmem, vmem, vmem],
         out_specs=(hbm, hbm),
-        scratch_shapes=[pltpu.VMEM(tiled, bf16), dma((chunks // GROUP,)), dma],
+        scratch_shapes=[pltpu.VMEM(tiled, bf16), dma, dma],
         compiler_params=pltpu.CompilerParams(vmem_limit_bytes=16 << 20),
         name="residual",
     )(merged, left, right, factor)

time: 35.5 us -> 32.7 us (0.921)
  Pallas kernels: 34.8 us -> 31.9 us
    pallas_call x1, Pallas kernels: 31.8 us -> 29.8 us  [per_device(): pl.pallas_call(functools.partial(factor_kernel, chunks), out_shape=(pltpu...]
    pallas_call x1, Pallas kernels: 2.98 us -> 2.14 us  [per_device(): pl.pallas_call(functools.partial(residual_kernel, chunks), out_shape=(plt...]
where the time goes in v4:
time: 32.7 us; the launch traced here: 32.5 us
  Pallas kernels  31.9 us (98%)
  between operations  0.64 us (2%)
    pallas_call x1, Pallas kernels, per_device(): pl.pallas_call(functools.partial(factor_kernel, chunks), out_shape=(pltpu...  29.8 us
    pallas_call x1, Pallas kernels, per_device(): pl.pallas_call(functools.partial(residual_kernel, chunks), out_shape=(plt...  2.14 us

profile of v4, /device:TPU:1, one launch (start us, length us, event | category | flops | bytes accessed | tf_op | source)
XLA Modules:
  0.0 32.5 jit_solution(10568245962097605098)
XLA Ops:
  0.6 29.8 %factor.1 = (f32[27,512,128]{2,1,0:T(8,128)S(1)}, bf16[27,128,32]{2,1,0:T(8,128)(2,1)S(1)}, bf16[32,512]{1,0:T(8,128)(2,1)S(1)}, f32[4,128]{1,0:T(4,128)S(1)}) custom-call(bf16[27,512,128]{2,1,0:T(8,128)(2,1)} %bitcast.5, bf16[27,512,128]{2,1,0:T(8,128)(2,1)} %bitcast.6, f32[4,128]{1,0:T(4,128)} %bitcast.7), custom_call_target="tpu_custom_call" | custom-call | tf_op jit(solution)/shard_map/factor/pallas_call | solution.py:368
  30.4 2.1 %residual.1 = (bf16[27,512,128]{2,1,0:T(8,128)(2,1)}, f32[4,128]{1,0:T(4,128)}) custom-call(f32[27,512,128]{2,1,0:T(8,128)S(1)} %get-tuple-element.8.m_ref, bf16[27,128,32]{2,1,0:T(8,128)(2,1)S(1)} %get-tuple-element.9.left_ref, bf16[32,512]{1,0:T(8,128)(2,1)S(1)} %get-tuple-element.10.right_ref, f32[4,128]{1,0:T(4,128)S(1)} %get-tuple-element.11.factor_ref), custom_call_target="tpu_custom_call" | custom-call | tf_op jit(solution)/shard_map/residual/pallas_call | solution.py:397

commit v5 on v4

--- a/solution.py
+++ b/solution.py
@@ -77,7 +77,7 @@
 
 def factor_kernel(
     chunks, g_hbm, e_hbm, q_hbm, m_ref, left_ref, right_ref, factor_ref,
-    ge, q_ref, outgoing, arrived, deep, whole, terms, result_ref,
+    ge, rounded, q_ref, outgoing, arrived, deep, whole, terms, result_ref,
     load_sem, q_sem, rs_send, rs_recv, z_send, z_recv, ag_send, ag_recv, dp_send, dp_recv,
 ):
     y, x, core, z = place()
@@ -96,20 +96,9 @@
     def loads(step):
         at = pl.ds(group_at(step) * GROUP, GROUP)
         return [
-            pltpu.make_async_copy(src.at[at], ge.at[i, at], load_sem.at[step // 2])
+            pltpu.make_async_copy(src.at[at], ge.at[i, at], load_sem.at[max(step // 2, step - EARLY // 2)])
             for i, src in enumerate((g_hbm, e_hbm))
         ]
-
-    def side_by_side(bases):
-        return jnp.concatenate(
-            [
-                jnp.concatenate(
-                    [ge[i, pl.ds(base, GROUP)].reshape(GROUP * CHUNK, LANES) for i in range(2)], axis=1
-                )
-                for base in bases
-            ],
-            axis=0,
-        )
 
     q_copy = pltpu.make_async_copy(q_hbm, q_ref, q_sem)
     q_copy.start()
@@ -141,15 +130,23 @@
     q = q_ref[...]
     high = q.astype(jnp.bfloat16).astype(jnp.float32)
     both = jnp.concatenate([high, q - high], axis=0)
-    q_rows = jnp.concatenate([both, both], axis=1).astype(jnp.bfloat16)
+    q_rows = both.astype(jnp.bfloat16)
     upper = column_rows((2 * RANK, LANES)) < RANK
 
-    def project(pair, count):
-        bases = [group_at(2 * pair + i) * GROUP for i in range(count)]
+    def rows_of(bases):
+        return jnp.concatenate(
+            [rounded[pl.ds(base, GROUP)].reshape(GROUP * CHUNK, LANES) for base in bases], axis=0
+        )
+
+    def project(first, count, sem):
+        bases = [group_at(first + i) * GROUP for i in range(count)]
         done = ge.at[:, pl.ds(0, count * GROUP)]
-        pltpu.make_async_copy(done, done, load_sem.at[pair]).wait()
+        pltpu.make_async_copy(done, done, load_sem.at[sem]).wait()
+        for base in bases:
+            at = pl.ds(base, GROUP)
+            rounded[at] = ge[0, at] + ge[1, at]
         product = lax.dot_general(
-            q_rows, side_by_side(bases), (((1,), (1,)), ((), ())), preferred_element_type=jnp.float32
+            q_rows, rows_of(bases), (((1,), (1,)), ((), ())), preferred_element_type=jnp.float32
         )
         total = product + pltpu.roll(product, RANK, 0)
         for i in range(count * GROUP):
@@ -161,7 +158,7 @@
             outgoing[bases[i // GROUP] + i % GROUP] = tile.astype(jnp.bfloat16)
 
     def project_pair(pair, carry):
-        project(pair, 2)
+        project(2 * pair, 2, pair)
         return carry
 
     lax.fori_loop(0, EARLY // 2, project_pair, 0)
@@ -182,10 +179,9 @@
         return carry
 
     lax.fori_loop(0, EARLY, send_terms, 0)
-    for pair in range(EARLY // 2, pl.cdiv(groups, 2)):
-        count = min(2, groups - 2 * pair)
-        project(pair, count)
-        lax.fori_loop(2 * pair, 2 * pair + count, send_terms, 0)
+    for step in range(EARLY, groups):
+        project(step, 1, step - EARLY // 2)
+        send_terms(step, 0)
 
     @pl.when(owner)
     def _():
@@ -247,7 +243,7 @@
                 tile = whole[base + i].astype(jnp.float32)
                 left += [jnp.where(block_of == b, tile, 0.0).astype(jnp.bfloat16) for b in range(BLOCKS)]
         result_ref[...] += jnp.dot(
-            jnp.concatenate(left, axis=1), side_by_side(bases), preferred_element_type=jnp.float32
+            jnp.concatenate(left, axis=1), rows_of(bases), preferred_element_type=jnp.float32
         )
 
     def contract_pair(step, carry):
@@ -259,8 +255,7 @@
     lax.fori_loop(1, groups // 2 + 1, contract_pair, 0)
     result = result_ref[...]
 
-    half = result[:, :LANES] + result[:, LANES:]
-    half = half[: 2 * RANK] + half[2 * RANK :]
+    half = result[: 2 * RANK] + result[2 * RANK :]
     terms[dp] = half + pltpu.roll(half, RANK, 0)
     replicas = beside + [device(y, x, core, z_other)] + [device(y, xs[step], core, z) for step in (2, 1, 3)]
     for peer in replicas:
@@ -377,20 +372,21 @@
         out_specs=(vmem, vmem, vmem, vmem),
         scratch_shapes=[
             pltpu.VMEM((2, *tiled), bf16),
+            pltpu.VMEM(tiled, bf16),
             pltpu.VMEM((RANK, width), f32),
             pltpu.VMEM((chunks, TILE, LANES), bf16),
             pltpu.VMEM((PLANE, TILE, LANES), bf16),
             pltpu.VMEM((DEPTH, TILE, LANES), bf16),
             pltpu.VMEM((chunks, TILE, LANES), bf16),
             pltpu.VMEM((REPLICAS, 2 * RANK, LANES), f32),
-            pltpu.VMEM((TILE, 2 * LANES), f32),
-            dma((pl.cdiv(chunks // GROUP, 2),)),
+            pltpu.VMEM((TILE, LANES), f32),
+            dma((chunks // GROUP - EARLY // 2,)),
             dma, dma, dma, dma, dma, dma,
             dma((chunks // GROUP,)),
             dma, dma,
         ],
         compiler_params=pltpu.CompilerParams(
-            collective_id=0, has_side_effects=True, vmem_limit_bytes=24 << 20
+            collective_id=0, has_side_effects=True, vmem_limit_bytes=28 << 20
         ),
         name="factor",
     )(*operands)

time: 32.7 us -> 32.2 us (0.985)
  Pallas kernels: 31.9 us -> 31.4 us
    pallas_call x1, Pallas kernels: 29.8 us -> 29.3 us  [per_device(): pl.pallas_call(functools.partial(factor_kernel, chunks), out_shape=(pltpu...]
where the time goes in v5:
time: 32.2 us; the launch traced here: 32.1 us
  Pallas kernels  31.4 us (98%)
  between operations  0.64 us (2%)
    pallas_call x1, Pallas kernels, per_device(): pl.pallas_call(functools.partial(factor_kernel, chunks), out_shape=(pltpu...  29.3 us
    pallas_call x1, Pallas kernels, per_device(): pl.pallas_call(functools.partial(residual_kernel, chunks), out_shape=(plt...  2.15 us

profile of v5, /device:TPU:1, one launch (start us, length us, event | category | flops | bytes accessed | tf_op | source)
XLA Modules:
  0.0 32.1 jit_solution(4596153004866793479)
XLA Ops:
  0.6 29.3 %factor.1 = (f32[27,512,128]{2,1,0:T(8,128)S(1)}, bf16[27,128,32]{2,1,0:T(8,128)(2,1)S(1)}, bf16[32,512]{1,0:T(8,128)(2,1)S(1)}, f32[4,128]{1,0:T(4,128)S(1)}) custom-call(bf16[27,512,128]{2,1,0:T(8,128)(2,1)} %bitcast.5, bf16[27,512,128]{2,1,0:T(8,128)(2,1)} %bitcast.6, f32[4,128]{1,0:T(4,128)} %bitcast.7), custom_call_target="tpu_custom_call" | custom-call | tf_op jit(solution)/shard_map/factor/pallas_call | solution.py:363
  29.9 2.1 %residual.1 = (bf16[27,512,128]{2,1,0:T(8,128)(2,1)}, f32[4,128]{1,0:T(4,128)}) custom-call(f32[27,512,128]{2,1,0:T(8,128)S(1)} %get-tuple-element.8.m_ref, bf16[27,128,32]{2,1,0:T(8,128)(2,1)S(1)} %get-tuple-element.9.left_ref, bf16[32,512]{1,0:T(8,128)(2,1)S(1)} %get-tuple-element.10.right_ref, f32[4,128]{1,0:T(4,128)S(1)} %get-tuple-element.11.factor_ref), custom_call_target="tpu_custom_call" | custom-call | tf_op jit(solution)/shard_map/residual/pallas_call | solution.py:393

commit v6 on v5

--- a/solution.py
+++ b/solution.py
@@ -19,7 +19,6 @@
 DEPTH = 8
 REPLICAS = 8
 AHEAD = 2
-UNROLL = 3
 EARLY = 6
 
 
@@ -46,8 +45,18 @@
     return {"head": (y * 4 + div(z, 2)) * 2 + core, "dp": rem(z, 2) * 4 + x}
 
 
+def turned(row, column):
+    return column + rem(row, 2) * (3 - 2 * column)
+
+
+def number_of(y, x, core):
+    row = wrap(y + 3, 4)
+    return (row * 4 + turned(row, x)) * 2 + core
+
+
 def of_plane(index, z):
-    return device(div(index, 8), rem(div(index, 2), 4), rem(index, 2), z)
+    row = div(index, 8)
+    return device(wrap(row + 1, 4), turned(row, rem(div(index, 2), 4)), rem(index, 2), z)
 
 
 def column_rows(shape):
@@ -81,7 +90,7 @@
     load_sem, q_sem, rs_send, rs_recv, z_send, z_recv, ag_send, ag_recv, dp_send, dp_recv,
 ):
     y, x, core, z = place()
-    me = (y * 4 + x) * 2 + core
+    me = number_of(y, x, core)
     dp = rem(z, 2) * 4 + x
     owner = me < chunks
     groups = chunks // GROUP
@@ -322,30 +331,15 @@
 
 
 def residual_kernel(chunks, m_ref, left_ref, right_ref, factor_ref, out_hbm, factor_hbm, out, sem, factor_sem):
-    groups = chunks // GROUP
     factor_copy = pltpu.make_async_copy(factor_ref, factor_hbm, factor_sem)
+
+    for chunk in range(chunks):
+        product = jnp.dot(left_ref[chunk], right_ref[...], preferred_element_type=jnp.float32)
+        for b in range(BLOCKS):
+            at = slice(b * LANES, (b + 1) * LANES)
+            out[chunk, at] = (m_ref[chunk, at] - product[:, at]).astype(jnp.bfloat16)
+        pltpu.make_async_copy(out.at[chunk], out_hbm.at[chunk], sem).start()
     factor_copy.start()
-
-    def stores(step):
-        at = pl.ds(step * GROUP, GROUP)
-        return pltpu.make_async_copy(out.at[at], out_hbm.at[at], sem)
-
-    def work(big, carry):
-        for small in range(UNROLL):
-            one(big * UNROLL + small)
-        return carry
-
-    def one(step):
-        for i in range(GROUP):
-            chunk = step * GROUP + i
-            product = jnp.dot(left_ref[chunk], right_ref[...], preferred_element_type=jnp.float32)
-            for b in range(BLOCKS):
-                at = slice(b * LANES, (b + 1) * LANES)
-                out[chunk, at] = (m_ref[chunk, at] - product[:, at]).astype(jnp.bfloat16)
-        stores(step).start()
-
-    lax.fori_loop(0, groups // UNROLL, work, 0)
-
     pltpu.make_async_copy(out, out_hbm, sem).wait()
     factor_copy.wait()
 

time: 32.2 us -> 31.7 us (0.984)
  Pallas kernels: 31.4 us -> 31 us
where the time goes in v6:
time: 31.7 us; the launch traced here: 31.6 us
  Pallas kernels  31 us (98%)
  between operations  0.64 us (2%)
    pallas_call x1, Pallas kernels, per_device(): pl.pallas_call(functools.partial(factor_kernel, chunks), out_shape=(pltpu...  29.1 us
    pallas_call x1, Pallas kernels, per_device(): pl.pallas_call(functools.partial(residual_kernel, chunks), out_shape=(plt...  1.95 us

profile of v6, /device:TPU:1, one launch (start us, length us, event | category | flops | bytes accessed | tf_op | source)
XLA Modules:
  0.0 31.6 jit_solution(13546290037584723107)
XLA Ops:
  0.6 29.1 %factor.1 = (f32[27,512,128]{2,1,0:T(8,128)S(1)}, bf16[27,128,32]{2,1,0:T(8,128)(2,1)S(1)}, bf16[32,512]{1,0:T(8,128)(2,1)S(1)}, f32[4,128]{1,0:T(4,128)S(1)}) custom-call(bf16[27,512,128]{2,1,0:T(8,128)(2,1)} %bitcast.5, bf16[27,512,128]{2,1,0:T(8,128)(2,1)} %bitcast.6, f32[4,128]{1,0:T(4,128)} %bitcast.7), custom_call_target="tpu_custom_call" | custom-call | tf_op jit(solution)/shard_map/factor/pallas_call | solution.py:357
  29.7 1.9 %residual.1 = (bf16[27,512,128]{2,1,0:T(8,128)(2,1)}, f32[4,128]{1,0:T(4,128)}) custom-call(f32[27,512,128]{2,1,0:T(8,128)S(1)} %get-tuple-element.8.m_ref, bf16[27,128,32]{2,1,0:T(8,128)(2,1)S(1)} %get-tuple-element.9.left_ref, bf16[32,512]{1,0:T(8,128)(2,1)S(1)} %get-tuple-element.10.right_ref, f32[4,128]{1,0:T(4,128)S(1)} %get-tuple-element.11.factor_ref), custom_call_target="tpu_custom_call" | custom-call | tf_op jit(solution)/shard_map/residual/pallas_call | solution.py:387

commit v7 on v6

--- a/solution.py
+++ b/solution.py
@@ -87,7 +87,24 @@
 def factor_kernel(
     chunks, g_hbm, e_hbm, q_hbm, m_ref, left_ref, right_ref, factor_ref,
     ge, rounded, q_ref, outgoing, arrived, deep, whole, terms, result_ref,
-    load_sem, q_sem, rs_send, rs_recv, z_send, z_recv, ag_send, ag_recv, dp_send, dp_recv,
+    rs_recv, z_recv, ag_recv, dp_recv,
+):
+    dma = pltpu.SemaphoreType.DMA
+    pl.run_scoped(
+        functools.partial(
+            factor_body, chunks, g_hbm, e_hbm, q_hbm, m_ref, left_ref, right_ref, factor_ref,
+            ge, rounded, q_ref, outgoing, arrived, deep, whole, terms, result_ref,
+            rs_recv, z_recv, ag_recv, dp_recv,
+        ),
+        dma((chunks // GROUP - EARLY // 2,)), dma, dma, dma, dma, dma,
+    )
+
+
+def factor_body(
+    chunks, g_hbm, e_hbm, q_hbm, m_ref, left_ref, right_ref, factor_ref,
+    ge, rounded, q_ref, outgoing, arrived, deep, whole, terms, result_ref,
+    rs_recv, z_recv, ag_recv, dp_recv,
+    load_sem, q_sem, rs_send, z_send, ag_send, dp_send,
 ):
     y, x, core, z = place()
     me = number_of(y, x, core)
@@ -129,13 +146,15 @@
 
     barrier = pltpu.get_barrier_semaphore()
     greeted = plane + line + beside
-    for peer in greeted:
+    for peer in plane:
         pl.semaphore_signal(barrier, inc=1, device_id=peer, device_id_type=MESH)
 
     q_copy.wait()
     for step in range(AHEAD, groups):
         for copy in loads(step):
             copy.start()
+    for peer in line + beside:
+        pl.semaphore_signal(barrier, inc=1, device_id=peer, device_id_type=MESH)
     q = q_ref[...]
     high = q.astype(jnp.bfloat16).astype(jnp.float32)
     both = jnp.concatenate([high, q - high], axis=0)
@@ -374,10 +393,10 @@
             pltpu.VMEM((chunks, TILE, LANES), bf16),
             pltpu.VMEM((REPLICAS, 2 * RANK, LANES), f32),
             pltpu.VMEM((TILE, LANES), f32),
-            dma((chunks // GROUP - EARLY // 2,)),
-            dma, dma, dma, dma, dma, dma,
+            dma,
+            dma,
             dma((chunks // GROUP,)),
-            dma, dma,
+            dma,
         ],
         compiler_params=pltpu.CompilerParams(
             collective_id=0, has_side_effects=True, vmem_limit_bytes=28 << 20

time: 31.7 us -> 31.7 us (level)
  no operation moved by 1% of the time
where the time goes in v7:
time: 31.7 us; the launch traced here: 31.6 us
  Pallas kernels  30.9 us (97%)
  between operations  0.64 us (2%)
    pallas_call x1, Pallas kernels, per_device(): pl.pallas_call(functools.partial(factor_kernel, chunks), out_shape=(pltpu...  29 us
    pallas_call x1, Pallas kernels, per_device(): pl.pallas_call(functools.partial(residual_kernel, chunks), out_shape=(plt...  1.96 us

profile of v7, /device:TPU:1, one launch (start us, length us, event | category | flops | bytes accessed | tf_op | source)
XLA Modules:
  0.0 31.6 jit_solution(1599018141552108113)
XLA Ops:
  0.6 29.0 %factor.1 = (f32[27,512,128]{2,1,0:T(8,128)S(1)}, bf16[27,128,32]{2,1,0:T(8,128)(2,1)S(1)}, bf16[32,512]{1,0:T(8,128)(2,1)S(1)}, f32[4,128]{1,0:T(4,128)S(1)}) custom-call(bf16[27,512,128]{2,1,0:T(8,128)(2,1)} %bitcast.5, bf16[27,512,128]{2,1,0:T(8,128)(2,1)} %bitcast.6, f32[4,128]{1,0:T(4,128)} %bitcast.7), custom_call_target="tpu_custom_call" | custom-call | tf_op jit(solution)/shard_map/factor/pallas_call | solution.py:376
  29.6 2.0 %residual.1 = (bf16[27,512,128]{2,1,0:T(8,128)(2,1)}, f32[4,128]{1,0:T(4,128)}) custom-call(f32[27,512,128]{2,1,0:T(8,128)S(1)} %get-tuple-element.8.m_ref, bf16[27,128,32]{2,1,0:T(8,128)(2,1)S(1)} %get-tuple-element.9.left_ref, bf16[32,512]{1,0:T(8,128)(2,1)S(1)} %get-tuple-element.10.right_ref, f32[4,128]{1,0:T(4,128)S(1)} %get-tuple-element.11.factor_ref), custom_call_target="tpu_custom_call" | custom-call | tf_op jit(solution)/shard_map/residual/pallas_call | solution.py:406

commit v8 on v7

--- a/solution.py
+++ b/solution.py
@@ -18,7 +18,7 @@
 PLANE = 32
 DEPTH = 8
 REPLICAS = 8
-AHEAD = 2
+AHEAD = 3
 EARLY = 6
 
 
@@ -285,7 +285,8 @@
 
     half = result[: 2 * RANK] + result[2 * RANK :]
     terms[dp] = half + pltpu.roll(half, RANK, 0)
-    replicas = beside + [device(y, x, core, z_other)] + [device(y, xs[step], core, z) for step in (2, 1, 3)]
+    beside_here = [device(y, xs[step], core, z) for step in (2, 1, 3)]
+    replicas = beside + beside_here[:1] + [device(y, x, core, z_other)] + beside_here[1:]
     for peer in replicas:
         pltpu.make_async_remote_copy(
             src_ref=terms.at[dp], dst_ref=terms.at[dp], send_sem=dp_send, recv_sem=dp_recv,

time: 31.7 us -> 31.7 us (level)
  no operation moved by 1% of the time
where the time goes in v8:
time: 31.7 us; the launch traced here: 31.6 us
  Pallas kernels  31 us (98%)
  between operations  0.64 us (2%)
    pallas_call x1, Pallas kernels, per_device(): pl.pallas_call(functools.partial(factor_kernel, chunks), out_shape=(pltpu...  29 us
    pallas_call x1, Pallas kernels, per_device(): pl.pallas_call(functools.partial(residual_kernel, chunks), out_shape=(plt...  1.95 us

profile of v8, /device:TPU:1, one launch (start us, length us, event | category | flops | bytes accessed | tf_op | source)
XLA Modules:
  0.0 31.6 jit_solution(9339413954197648277)
XLA Ops:
  0.6 29.0 %factor.1 = (f32[27,512,128]{2,1,0:T(8,128)S(1)}, bf16[27,128,32]{2,1,0:T(8,128)(2,1)S(1)}, bf16[32,512]{1,0:T(8,128)(2,1)S(1)}, f32[4,128]{1,0:T(4,128)S(1)}) custom-call(bf16[27,512,128]{2,1,0:T(8,128)(2,1)} %bitcast.5, bf16[27,512,128]{2,1,0:T(8,128)(2,1)} %bitcast.6, f32[4,128]{1,0:T(4,128)} %bitcast.7), custom_call_target="tpu_custom_call" | custom-call | tf_op jit(solution)/shard_map/factor/pallas_call | solution.py:377
  29.6 1.9 %residual.1 = (bf16[27,512,128]{2,1,0:T(8,128)(2,1)}, f32[4,128]{1,0:T(4,128)}) custom-call(f32[27,512,128]{2,1,0:T(8,128)S(1)} %get-tuple-element.8.m_ref, bf16[27,128,32]{2,1,0:T(8,128)(2,1)S(1)} %get-tuple-element.9.left_ref, bf16[32,512]{1,0:T(8,128)(2,1)S(1)} %get-tuple-element.10.right_ref, f32[4,128]{1,0:T(4,128)S(1)} %get-tuple-element.11.factor_ref), custom_call_target="tpu_custom_call" | custom-call | tf_op jit(solution)/shard_map/residual/pallas_call | solution.py:407
